TPU v7x, 32 devices: a whole 2x2x4 slice. The times are simulated.
32 devices in a mesh: mesh: 16 (over z, y, core), mem: 2 (over x).
Axes of the slice: x: 2, y: 2, z: 4, core: 2. Of those that a mesh axis runs over, the one named last changes fastest.
Arguments:
- ensemble: bfloat16 [40, 240, 6144], P('mem', None, 'mesh'), may hold values from -6 to 6
- ovl_owner: int32 [384, 2], P('mesh'), may hold values from 0 to 15, all different within a row; in each aligned block of 24 rows (0 to 23, 24 to 47, ...) at most 5 rows name the same one
- ovl_patch: int32 [384, 2], P('mesh'), may hold values from 0 to 7
- ovl_weight: bfloat16 [384, 2, 16, 8], P('mesh'), may hold values from 0.0099487305 to 0.19921875
- letkf_weight: float32 [16, 40, 40], P('mesh'), may hold values from -1 to 1
Outputs:
- analysis: bfloat16 [40, 240, 6144], P('mem', None, 'mesh')
Inputs may be any that keep to these rules, and one draw needn't show every extreme that they name: `ovl_owner`: within the 24 rows of one mesh index, the two entries of a row differ, and each owner is named at most 5 times; some owner exactly 5 times.
All inputs are finite; a program needn't handle non-finite values.
Results may differ from a plain program's by a relative error of at most 0.0015.
Values may be sent and summed in bfloat16 or wider, within the bound.
A program may use at most 128 MiB of HBM per device.

v0:
```python
import jax
import jax.numpy as jnp
from jax import lax
from jax.sharding import PartitionSpec as P

PATCH_TILE = 8


def patch_grid(contribution, slot_margin, slot_codes, patch_count):
    slot_total = contribution.shape[0]
    assign = (
        jnp.arange(1, patch_count + 1, dtype=jnp.int32)[:, None]
        == slot_codes.reshape(-1).astype(jnp.int32)[None, :]
    )
    assign_half = assign.astype(jnp.bfloat16)
    patch_sums = jnp.dot(
        assign_half, contribution.reshape(slot_total, -1), preferred_element_type=jnp.float32
    )
    patch_sums = patch_sums.reshape((patch_count,) + contribution.shape[1:])
    column_sums = jnp.sum(slot_margin.astype(jnp.float32), axis=1)
    coverage = jnp.dot(assign.astype(jnp.float32), column_sums, precision=lax.Precision.HIGHEST)
    grid_field = (patch_sums / jnp.maximum(coverage, 1.0)[:, :, None, None]).astype(jnp.bfloat16)
    return (grid_field, assign_half)


def shards(ensemble, ovl_owner, ovl_patch, ovl_weight, letkf_weight):
    members, channels, element_count = ensemble.shape
    block_count = ovl_owner.shape[0]
    block_size = ovl_weight.shape[2]
    cell_count = ovl_weight.shape[3]
    tile_count = letkf_weight.shape[0]
    patch_count = tile_count * PATCH_TILE
    peer_count = lax.axis_size("mesh")
    capacity = max(2, (3 * block_count + peer_count - 1) // peer_count)
    slot_total = peer_count * capacity
    piece_count = 2 * block_count
    blocks = ensemble.reshape(members, channels, block_count, block_size)
    owners = ovl_owner.reshape(-1)
    patches = ovl_patch.reshape(-1)
    positions = jnp.arange(piece_count, dtype=jnp.int32)
    same_owner = owners[:, None] == owners[None, :]
    earlier = positions[:, None] > positions[None, :]
    ranking = jnp.sum(jnp.where(same_owner & earlier, 1, 0), axis=1).astype(jnp.int32)
    slot_index = owners * capacity + ranking
    selector = (jnp.arange(slot_total, dtype=jnp.int32)[:, None] == slot_index[None, :]).astype(
        jnp.bfloat16
    )
    codes = (patches + 1).astype(jnp.bfloat16)[:, None]
    slot_codes = (
        jnp.dot(selector, codes, preferred_element_type=jnp.float32)
        .astype(jnp.bfloat16)
        .reshape(peer_count, capacity)
    )
    weight_flat = ovl_weight.reshape(piece_count, block_size * cell_count)
    slot_weight = jnp.dot(selector, weight_flat, preferred_element_type=jnp.float32).astype(
        jnp.bfloat16
    )
    slot_weight = slot_weight.reshape(peer_count, capacity, block_size * cell_count)
    formed = jnp.einsum("mcbe,bkeg->bkgmc", blocks, ovl_weight, preferred_element_type=jnp.float32)
    payload = formed.astype(jnp.bfloat16).reshape(piece_count, -1)
    slot_data = jnp.dot(selector, payload, preferred_element_type=jnp.float32).astype(jnp.bfloat16)
    slot_data = slot_data.reshape(peer_count, capacity, -1)
    got_data, got_weight, got_codes = (
        lax.all_to_all(slot_data, "mesh", split_axis=0, concat_axis=0, tiled=True),
        lax.all_to_all(slot_weight, "mesh", split_axis=0, concat_axis=0, tiled=True),
        lax.all_to_all(slot_codes, "mesh", split_axis=0, concat_axis=0, tiled=True),
    )
    slot_margin = got_weight.reshape(slot_total, block_size, cell_count)
    contribution = got_data.reshape(slot_total, cell_count, members, channels)
    grid_field, assign_half = patch_grid(contribution, slot_margin, got_codes, patch_count)
    tile_view = grid_field.reshape(tile_count, PATCH_TILE, cell_count, members, channels)
    own_start = lax.axis_index("mem") * members
    own_cols = lax.dynamic_slice_in_dim(letkf_weight, own_start, members, 2)
    mixed = jnp.einsum(
        "tjgmc,tmn->tjgnc",
        lax.all_gather(tile_view, "mem", axis=3, tiled=True).astype(jnp.float32),
        own_cols,
        precision=lax.Precision.HIGHEST,
    )
    increment = (mixed - tile_view.astype(jnp.float32)).astype(jnp.bfloat16)
    increment_flat = increment.reshape(patch_count, -1)
    send_back = jnp.dot(assign_half.T, increment_flat, preferred_element_type=jnp.float32).astype(
        jnp.bfloat16
    )
    send_back = send_back.reshape(peer_count, capacity, -1)
    returned = lax.all_to_all(send_back, "mesh", split_axis=0, concat_axis=0, tiled=True)
    returned_flat = returned.reshape(slot_total, -1)
    own_pieces = jnp.dot(selector.T, returned_flat, preferred_element_type=jnp.float32).astype(
        jnp.bfloat16
    )
    own_pieces = own_pieces.reshape(block_count, 2, cell_count, members, channels)
    element_area = jnp.sum(ovl_weight.astype(jnp.float32), axis=(1, 3))
    correction = jnp.einsum(
        "bkgmc,bkeg->mcbe", own_pieces, ovl_weight, preferred_element_type=jnp.float32
    )
    correction = correction / element_area[None, None]
    updated = (blocks.astype(jnp.float32) + correction).astype(jnp.bfloat16)
    return updated.reshape(members, channels, element_count)


def solution(mesh):
    in_specs = (
        P("mem", None, "mesh"),
        P("mesh", None),
        P("mesh", None),
        P("mesh", None, None, None),
        P("mesh", None, None),
    )
    out_specs = P("mem", None, "mesh")
    return jax.shard_map(shards, mesh=mesh, in_specs=in_specs, out_specs=out_specs, check_vma=False)
```

profile of v0, /device:TPU:13, one launch (start us, length us, event | category | flops | bytes accessed | tf_op | source)
XLA Modules:
  0.0 632.3 jit_solution(10530939711568154724)
XLA Ops:
  6.5 0.8 copy.55
  7.6 0.7 add_convert_fusion
  8.6 0.7 all_to_all.20
  9.3 6.5 %all-to-all-start = ((bf16[16,1,5]{2,1,0:T(2,128)(2,1)}), bf16[16,1,5]{2,1,0:T(2,128)(2,1)S(1)}, u32[]{:S(2)}, u32[]{:S(2)}) async-start(bf16[16,1,5]{2,1,0:T(2,128)(2,1)} %all_to_all.20), calls=%async_computation | async-start | bytes 16384 | tf_op jit(solution)/shard_map/all_to_all | solution.py:66
  15.9 1.2 copy.63
  17.3 6.1 copy.53
  23.5 5.2 fusion.7
  28.8 0.6 reshape.95
  29.4 5.7 copy.61
  35.1 8.9 %reshape.92 = bf16[48,38400]{1,0:T(8,128)(2,1)} reshape(bf16[24,2,8,20,240]{4,3,2,1,0:T(8,128)(2,1)} %copy.61) | data formatting | bytes 7372800 | tf_op jit(solution)/shard_map/reshape | solution.py:60
  44.0 6.0 all-to-all-start.2
  50.0 6.3 convolution_convert_fusion.1
  56.3 11.1 %reshape.93 = bf16[16,5,38400]{2,1,0:T(8,128)(2,1)} reshape(bf16[80,38400]{1,0:T(8,128)(2,1)} %convolution_convert_fusion.1) | data formatting | bytes 12288000 | tf_op jit(solution)/shard_map/reshape | solution.py:62
  67.3 6.0 all-to-all-start.1
  74.5 212.1 %all-to-all-done.1 = bf16[16,5,38400]{2,1,0:T(8,128)(2,1)} async-done(((bf16[16,5,38400]{2,1,0:T(8,128)(2,1)}), bf16[16,5,38400]{2,1,0:T(8,128)(2,1)}, u32[]{:S(2)}, u32[]{:S(2)}) %all-to-all-start.1) | async-done | bytes 6144032 | tf_op jit(solution)/shard_map/all_to_all | solution.py:64
  286.6 10.9 %reshape_reshape.3 = bf16[80,38400]{1,0:T(8,128)(2,1)} reshape(bf16[16,5,38400]{2,1,0:T(8,128)(2,1)} %all-to-all-done.1) | data formatting | bytes 12288000 | tf_op jit(solution)/shard_map/reshape;reshape | solution.py:17
  297.5 16.3 %dot_general.40 = bf16[8,20,240,80]{2,1,0,3:T(8,128)(2,1)} reshape(bf16[38400,80]{0,1:T(8,128)(2,1)} %bitcast.52) | data formatting | bytes 12288000 | tf_op jit(solution)/shard_map/dot_general | solution.py:16
  313.8 7.6 %divide_convert_fusion = bf16[8,8,20,240]{3,0,2,1:T(8,128)(2,1)} fusion(bf16[8,20,240,80]{2,1,0,3:T(8,128)(2,1)} %dot_general.40, f32[8,8]{0,1:T(8,128)S(1)} %copy.64, s32[80]{0:T(128)S(1)} %reshape.103, s32[8]{0:T(128)S(1)} %iota_add_fusion), kind=kOutput, calls=%fused_computation.17 | convolution fusion | flops 49767040 | bytes 6759008 | tf_op jit(solution)/shard_map/dot_general | solution.py:16
  321.5 23.6 %all-gather.3.cloned.1.call-done = bf16[8,8,40,240]{3,0,2,1:T(8,128)(2,1)} async-done(((bf16[8,8,20,240]{3,0,2,1:T(8,128)(2,1)}), bf16[8,8,40,240]{3,0,2,1:T(8,128)(2,1)}) %all-gather.3.cloned.1.call-update) | async-done | bytes 1228816 | tf_op jit(solution)/shard_map/all_gather | solution.py:76
  345.1 2.4 fusion.13
  347.5 0.8 fusion.12
  348.5 1.0 reshape.98
  349.5 4.4 convolution_convert_fusion
  353.9 10.9 %reshape.99 = bf16[16,5,38400]{2,1,0:T(8,128)(2,1)} reshape(bf16[80,38400]{1,0:T(8,128)(2,1)} %convolution_convert_fusion) | data formatting | bytes 12288000 | tf_op jit(solution)/shard_map/reshape | solution.py:85
  364.8 6.5 %all-to-all-start.3 = ((bf16[16,5,38400]{2,1,0:T(8,128)(2,1)}), bf16[16,5,38400]{2,1,0:T(8,128)(2,1)}, u32[]{:S(2)}, u32[]{:S(2)}) async-start(bf16[16,5,38400]{2,1,0:T(8,128)(2,1)} %reshape.99), calls=%async_computation.3 | async-start | bytes 19660800 | tf_op jit(solution)/shard_map/all_to_all | solution.py:86
  371.6 213.0 %all-to-all-done.3 = bf16[16,5,38400]{2,1,0:T(8,128)(2,1)} async-done(((bf16[16,5,38400]{2,1,0:T(8,128)(2,1)}), bf16[16,5,38400]{2,1,0:T(8,128)(2,1)}, u32[]{:S(2)}, u32[]{:S(2)}) %all-to-all-start.3) | async-done | bytes 6144032 | tf_op jit(solution)/shard_map/all_to_all | solution.py:86
  584.5 10.8 %reshape.100 = bf16[80,38400]{1,0:T(8,128)(2,1)} reshape(bf16[16,5,38400]{2,1,0:T(8,128)(2,1)} %all-to-all-done.3) | data formatting | bytes 12288000 | tf_op jit(solution)/shard_map/reshape | solution.py:87
  595.3 5.8 convolution_convert_fusion.2
  601.1 10.6 %reshape.101 = bf16[24,2,8,20,240]{4,3,2,1,0:T(8,128)(2,1)} reshape(bf16[48,38400]{1,0:T(8,128)(2,1)} %convolution_convert_fusion.2) | data formatting | bytes 7372800 | tf_op jit(solution)/shard_map/reshape | solution.py:91
  611.7 5.3 fusion
  617.0 2.3 copy.71
  619.3 6.2 copy.72
  (32 shorter events, 2.6 us)
Async XLA Ops:
  6.5 338.6 %copy-start = (f32[1,40,40]{2,1,0:T(8,128)S(1)}, f32[1,40,40]{2,1,0:T(8,128)}, u32[]{:S(2)}) copy-start(f32[1,40,40]{2,1,0:T(8,128)} %param.9) | copy-start | bytes 19204
  9.3 34.6 %all-to-all-start = ((bf16[16,1,5]{2,1,0:T(2,128)(2,1)}), bf16[16,1,5]{2,1,0:T(2,128)(2,1)S(1)}, u32[]{:S(2)}, u32[]{:S(2)}) async-start(bf16[16,1,5]{2,1,0:T(2,128)(2,1)} %all_to_all.20), calls=%async_computation | async-start | bytes 16384 | tf_op jit(solution)/shard_map/all_to_all | solution.py:66
  17.1 6.3 copy-start.3
  44.0 23.4 %all-to-all-start.2 = ((bf16[16,5,128]{2,1,0:T(8,128)(2,1)}), bf16[16,5,128]{2,1,0:T(8,128)(2,1)S(1)}, u32[]{:S(2)}, u32[]{:S(2)}) async-start(bf16[16,5,128]{2,1,0:T(8,128)(2,1)} %reshape.95), calls=%async_computation.2 | async-start | bytes 65536 | tf_op jit(solution)/shard_map/all_to_all | solution.py:65
  67.3 219.3 %all-to-all-start.1 = ((bf16[16,5,38400]{2,1,0:T(8,128)(2,1)}), bf16[16,5,38400]{2,1,0:T(8,128)(2,1)}, u32[]{:S(2)}, u32[]{:S(2)}) async-start(bf16[16,5,38400]{2,1,0:T(8,128)(2,1)} %reshape.93), calls=%async_computation.1 | async-start | bytes 19660800 | tf_op jit(solution)/shard_map/all_to_all | solution.py:64
  73.4 271.7 %all-gather.3.cloned.1.call-start = ((), (), s32[]{:S(2)}) async-start(), calls=%async_computation.4 | async-start | bytes 1966080 | tf_op jit(solution)/shard_map/all_gather | solution.py:76
  321.4 26.1 %copy-start.2 = (bf16[8,8,20,240]{3,0,2,1:T(8,128)(2,1)S(1)}, bf16[8,8,20,240]{3,0,2,1:T(8,128)(2,1)}, u32[]{:S(2)}) copy-start(bf16[8,8,20,240]{3,0,2,1:T(8,128)(2,1)} %divide_convert_fusion) | copy-start | bytes 1843204
  364.8 219.8 %all-to-all-start.3 = ((bf16[16,5,38400]{2,1,0:T(8,128)(2,1)}), bf16[16,5,38400]{2,1,0:T(8,128)(2,1)}, u32[]{:S(2)}, u32[]{:S(2)}) async-start(bf16[16,5,38400]{2,1,0:T(8,128)(2,1)} %reshape.99), calls=%async_computation.3 | async-start | bytes 19660800 | tf_op jit(solution)/shard_map/all_to_all | solution.py:86
  617.0 8.5 %copy-start.1 = (f32[1,40,40]{2,1,0:T(8,128)S(1)}, f32[1,40,40]{2,1,0:T(8,128)}, u32[]{:S(2)}) copy-start(f32[1,40,40]{2,1,0:T(8,128)} %param.9) | copy-start | bytes 19204
Sparse Core Ops, SparseCore 0:
  321.6 23.4 all-gather.2
where the time goes:
time: 634 us; the launch traced here: 632 us
  waiting for transfers between devices  449 us (71%)
  local copies, waits for them, and re-layouts  105 us (17%)
  matrix products  37.4 us (6%)
  starting transfers between devices  25.3 us (4%)
  between operations  13.6 us (2%)
    all_to_all x1, waiting for transfers between devices, shards(): lax.all_to_all(send_back, 'mesh', split_axis=0, concat_axis=0, tiled=True)  213 us
    all_to_all x1, waiting for transfers between devices, shards(): lax.all_to_all(slot_data, 'mesh', split_axis=0, concat_axis=0, tiled=True)  212 us
    all_gather x1, waiting for transfers between devices, shards(): lax.all_gather(tile_view, 'mem', axis=3, tiled=True).astype(jnp.float32)  23.6 us
    dot_general x1, local copies, waits for them, and re-layouts, patch_grid(): jnp.dot(assign_half, contribution.reshape(slot_total, -1), preferred_elem...  16.3 us
  transfers between devices with their start and end apart: 5, of which 3 were waited for; matrix products, arithmetic and copies ran while one was open for 7% of the time, Pallas kernels for 0%

commit v1 on v0

v1 whole, which is shorter than its diff:
```python
import jax
import jax.numpy as jnp
from jax import lax
from jax.sharding import PartitionSpec as P

PATCH_TILE = 8


def shards(ensemble, ovl_owner, ovl_patch, ovl_weight, letkf_weight):
    members, channels, element_count = ensemble.shape
    block_count = ovl_owner.shape[0]
    block_size = ovl_weight.shape[2]
    cell_count = ovl_weight.shape[3]
    tile_count = letkf_weight.shape[0]
    own_patches = tile_count * PATCH_TILE
    peer_count = lax.axis_size("mesh")
    patch_total = own_patches * peer_count
    width = members * channels
    flat = ensemble.reshape(width, element_count)

    dest = ovl_owner * own_patches + ovl_patch
    dest_elems = jnp.repeat(dest.T, block_size, axis=1)
    weight = ovl_weight.transpose(1, 3, 0, 2).reshape(2, cell_count, element_count)
    hits = jnp.arange(patch_total, dtype=jnp.int32)[None, :, None] == dest_elems[:, None, :]
    area = jnp.where(hits[0][:, None, :], weight[0][None], 0) + jnp.where(
        hits[1][:, None, :], weight[1][None], 0
    )
    area = area.reshape(patch_total * cell_count, element_count)

    cover_part = jnp.sum(area.astype(jnp.float32), axis=1)
    coverage = lax.psum_scatter(cover_part, "mesh", scatter_dimension=0, tiled=True)

    sums_part = lax.dot_general(
        area, flat, (((1,), (1,)), ((), ())), preferred_element_type=jnp.float32
    ).astype(jnp.bfloat16)
    patch_sums = lax.psum_scatter(sums_part, "mesh", scatter_dimension=0, tiled=True)
    grid_field = (patch_sums.astype(jnp.float32) / jnp.maximum(coverage, 1.0)[:, None]).astype(
        jnp.bfloat16
    )
    tile_view = grid_field.reshape(tile_count, PATCH_TILE * cell_count, members, channels)
    own_start = lax.axis_index("mem") * members
    own_cols = lax.dynamic_slice_in_dim(letkf_weight, own_start, members, 2)
    mixed = jnp.einsum(
        "trmc,tmn->trnc",
        lax.all_gather(tile_view, "mem", axis=2, tiled=True).astype(jnp.float32),
        own_cols,
        precision=lax.Precision.HIGHEST,
    )
    increment = (mixed - tile_view.astype(jnp.float32)).astype(jnp.bfloat16)
    everywhere = lax.all_gather(
        increment.reshape(own_patches * cell_count, width), "mesh", axis=0, tiled=True
    )
    element_area = jnp.sum(weight.astype(jnp.float32), axis=(0, 1))
    correction = lax.dot_general(
        everywhere, area, (((0,), (0,)), ((), ())), preferred_element_type=jnp.float32
    )
    updated = (flat.astype(jnp.float32) + correction / element_area[None]).astype(jnp.bfloat16)
    return updated.reshape(members, channels, element_count)


def solution(mesh):
    in_specs = (
        P("mem", None, "mesh"),
        P("mesh", None),
        P("mesh", None),
        P("mesh", None, None, None),
        P("mesh", None, None),
    )
    out_specs = P("mem", None, "mesh")
    return jax.shard_map(shards, mesh=mesh, in_specs=in_specs, out_specs=out_specs, check_vma=False)
```

time: 634 us -> 272 us (0.43)
  waiting for transfers between devices: 449 us -> 201 us
  local copies, waits for them, and re-layouts: 105 us -> 6 us
  starting transfers between devices: 25.3 us -> 0.09 us
  blocking collectives: 0 us -> 21.8 us
  matrix products: 37.4 us -> 22.8 us
    all_to_all x4 -> x0, waiting for transfers between devices: 425 us -> none  [the longest x1 213 us: shards(): lax.all_to_all(send_back, 'mesh', split_axis=0, concat_axis=0, tiled=True)]
    reduce_scatter x0 -> x1, waiting for transfers between devices: none -> 93.9 us  [shards(): lax.psum_scatter(sums_part, 'mesh', scatter_dimension=0, tiled=True)]
    all_gather x1 -> x2, waiting for transfers between devices: 23.6 us -> 107 us  [the longest x1 83.2 us: shards(): lax.all_gather(increment.reshape(own_patches * cell_count, width), 'mesh'...]
    reshape x10 -> x3, local copies, waits for them, and re-layouts: 60.3 us -> 3.76 us  [the longest x2 2.14 us: shards(): grid_field.reshape(tile_count, PATCH_TILE * cell_count, members, channels)]
    all_to_all x4 -> x0, starting transfers between devices: 25.1 us -> none  [the longest x1 6.52 us: shards(): lax.all_to_all(slot_codes, 'mesh', split_axis=0, concat_axis=0, tiled=True)]
    unnamed x0 -> x1, blocking collectives: none -> 21.8 us
    dot_general x1 -> x0, local copies, waits for them, and re-layouts: 16.3 us -> none  [patch_grid(): jnp.dot(assign_half, contribution.reshape(slot_total, -1), preferred_elem...]
    dot_general x10 -> x3, matrix products: 37.4 us -> 22.8 us  [the longest x1 10 us: shards(): lax.dot_general(area, flat, (((1,), (1,)), ((), ())), preferred_element_t...]
  transfers between devices with their start and end apart: 5 -> 3, of which waited for: 3 -> 3; matrix products, arithmetic and copies ran while one was open for 7% -> 1% of each run, Pallas kernels for 0% -> 0%
where the time goes in v1:
time: 272 us; the launch traced here: 268 us
  waiting for transfers between devices  201 us (74%)
  matrix products  22.8 us (8%)
  blocking collectives  21.8 us (8%)
  between operations  13.9 us (5%)
  local copies, waits for them, and re-layouts  6 us (2%)
    reduce_scatter x1, waiting for transfers between devices, shards(): lax.psum_scatter(sums_part, 'mesh', scatter_dimension=0, tiled=True)  93.9 us
    all_gather x1, waiting for transfers between devices, shards(): lax.all_gather(increment.reshape(own_patches * cell_count, width), 'mesh'...  83.2 us
    all_gather x1, waiting for transfers between devices, shards(): lax.all_gather(tile_view, 'mem', axis=2, tiled=True).astype(jnp.float32)  24.1 us
    unnamed x1, blocking collectives  21.8 us
    dot_general x1, matrix products, shards(): lax.dot_general(area, flat, (((1,), (1,)), ((), ())), preferred_element_t...  10 us
    dot_general x1, matrix products, shards(): lax.dot_general(everywhere, area, (((0,), (0,)), ((), ())), preferred_ele...  9.98 us
  transfers between devices with their start and end apart: 3, of which 3 were waited for; matrix products, arithmetic and copies ran while one was open for 1% of the time, Pallas kernels for 0%

profile of v1, /device:TPU:13, one launch (start us, length us, event | category | flops | bytes accessed | tf_op | source)
XLA Modules:
  0.0 268.4 jit_solution(16749443550250182540)
XLA Ops:
  6.5 0.7 add_bitcast_fusion
  7.2 0.1 broadcast_in_dim.45
  7.3 0.1 eq.16
  7.4 0.8 fusion.20
  8.2 0.1 copy.17
  8.3 0.1 broadcast_in_dim.48
  8.4 0.1 copy.18
  8.5 0.1 broadcast_in_dim.53
  8.6 0.1 iota_compare_fusion
  8.7 10.0 %convolution_convert_fusion = bf16[1024,4800]{1,0:T(8,128)(2,1)} fusion(bf16[4800,384]{1,0:T(8,128)(2,1)} %bitcast.37, pred[128,384]{1,0:T(8,128)(4,1)S(1)} %get-tuple-element.6, pred[128,384]{1,0:T(8,128)(4,1)S(1)} %get-tuple-element.5, bf16[8,384]{1,0:T(8,128)(2,1)S(1)} %broadcast_in_dim.53, bf16[8,384]{1,0:T(8,128)(2,1)S(1)} %broadcast_in_dim.48), kind=kOutput, calls=%fused_computation | convolution fusion | flops 3780968448 | bytes 13627392 | tf_op jit(solution)/shard_map/dot_general | solution.py:33
  18.8 0.0 reduce-scatter.2.cloned.1.call-update
  18.8 0.0 all-gather.3.cloned.1.call-start
  18.8 0.5 convert_reduce_fusion
  19.4 0.1 reduce_sum.21
  19.5 0.6 dynamic-slice
  20.7 21.8 %all-reduce = f32[1024]{0:T(1024)S(1)} all-reduce(f32[1024]{0:T(1024)S(1)} %reduce_sum.21), channel_id=3, replica_groups=mesh['mesh'=16,'mem'=2] {'mesh'}, use_global_device_ids=true, to_apply=%region_2.3.clone | all-reduce | flops 1024 | bytes 8192
  42.5 0.1 dynamic-slice_maximum_fusion
  42.6 93.9 %reduce-scatter.2.cloned.1.call-done = bf16[64,4800]{1,0:T(8,128)(2,1)} async-done(((bf16[1024,4800]{1,0:T(8,128)(2,1)}), bf16[64,4800]{1,0:T(8,128)(2,1)}) %reduce-scatter.2.cloned.1.call-update) | async-done | bytes 614416 | tf_op jit(solution)/shard_map/reduce_scatter | solution.py:36
  136.4 1.3 divide_convert_fusion
  137.7 1.2 reshape.72
  138.9 0.0 copy-start.1
  138.9 1.0 copy.19
  139.8 0.0 all-gather.3.cloned.1.call-update
  139.9 0.0 all-gather.5.cloned.1.call-start
  139.9 24.1 %all-gather.3.cloned.1.call-done = bf16[1,64,40,240]{3,1,0,2:T(8,128)(2,1)} async-done(((bf16[1,64,20,240]{3,1,0,2:T(8,128)(2,1)}), bf16[1,64,40,240]{3,1,0,2:T(8,128)(2,1)}) %all-gather.3.cloned.1.call-update) | async-done | bytes 1228816 | tf_op jit(solution)/shard_map/all_gather | solution.py:45
  164.1 2.8 %fusion = bf16[1,64,20,240]{3,2,1,0:T(8,128)(2,1)S(1)} fusion(bf16[1,64,20,240]{3,2,1,0:T(8,128)(2,1)S(1)} %reshape.72, bf16[1,64,40,240]{3,1,0,2:T(8,128)(2,1)} %all-gather.3.cloned.1.call-done, f32[1,40,40]{2,1,0:T(8,128)S(1)} %copy-done, s32[]{:T(128)S(6)} %select_n.30), kind=kOutput, calls=%fused_computation.3 | convolution fusion | flops 148377600 | bytes 2464004 | tf_op jit(solution)/shard_map/trmc,tmn->trnc/dot_general | solution.py:43
  166.9 1.6 reshape.74
  168.5 0.0 all-gather.5.cloned.1.call-update
  168.6 0.1 copy.21
  168.7 0.1 div.20
  168.7 83.2 %all-gather.5.cloned.1.call-done = bf16[1024,4800]{1,0:T(8,128)(2,1)} async-done(((bf16[64,4800]{1,0:T(8,128)(2,1)}), bf16[1024,4800]{1,0:T(8,128)(2,1)}) %all-gather.5.cloned.1.call-update) | async-done | bytes 9830416 | tf_op jit(solution)/shard_map/all_gather | solution.py:50
  251.9 10.0 %add_convert_fusion = bf16[4800,384]{1,0:T(8,128)(2,1)} fusion(bf16[4800,384]{1,0:T(8,128)(2,1)} %bitcast.38, bf16[1024,4800]{1,0:T(8,128)(2,1)} %all-gather.5.cloned.1.call-done, f32[384]{0:T(512)S(1)} %div.20, pred[128,384]{1,0:T(8,128)(4,1)S(1)} %get-tuple-element.6, pred[128,384]{1,0:T(8,128)(4,1)S(1)} %get-tuple-element.5, ...), kind=kOutput, calls=%fused_computation.1 | convolution fusion | flops 3783426048 | bytes 17315328 | tf_op jit(solution)/shard_map/dot_general | solution.py:54
  (8 shorter events, 0.1 us)
Async XLA Ops:
  6.5 157.5 %copy-start = (f32[1,40,40]{2,1,0:T(8,128)S(1)}, f32[1,40,40]{2,1,0:T(8,128)}, u32[]{:S(2)}) copy-start(f32[1,40,40]{2,1,0:T(8,128)} %param.9) | copy-start | bytes 19204
  6.5 129.9 %reduce-scatter.2.cloned.1.call-start = ((), (), s32[]{:S(2)}) async-start(), calls=%async_computation.1 | async-start | bytes 10584064 | tf_op jit(solution)/shard_map/reduce_scatter | solution.py:36
  18.8 0.7 copy-start.2
  18.8 145.3 %all-gather.3.cloned.1.call-start = ((), (), s32[]{:S(2)}) async-start(), calls=%async_computation.2 | async-start | bytes 1966080 | tf_op jit(solution)/shard_map/all_gather | solution.py:45
  138.9 29.7 %copy-start.1 = (bf16[24,2,16,8]{0,3,2,1:T(8,128)(2,1)S(1)}, bf16[24,2,16,8]{0,3,2,1:T(8,128)(2,1)}, u32[]{:S(2)}) copy-start(bf16[24,2,16,8]{0,3,2,1:T(8,128)(2,1)} %param.8) | copy-start | bytes 36868
  139.9 112.1 %all-gather.5.cloned.1.call-start = ((), (), s32[]{:S(2)}) async-start(), calls=%async_computation.3 | async-start | bytes 10584064 | tf_op jit(solution)/shard_map/all_gather | solution.py:50
Sparse Core Ops, SparseCore 0:
  18.9 117.4 reduce-scatter.1
  140.0 24.0 all-gather.2
  168.7 83.2 all-gather.4
